TPU v7x, 256 devices: a whole 4x4x8 slice. The times are simulated.
256 devices in a mesh: src: 16 (over z_lo, y), rcv: 16 (over z_hi, x, core).
Axes of the slice: x: 4, y: 4, z: 8 (z_hi: 2, z_lo: 4; z = z_hi * 4 + z_lo), core: 2. Of those that a mesh axis runs over, the one named last changes fastest.
Arguments:
- records: bfloat16 [4096, 8192], P(('rcv', 'src')), may hold values from -6 to 6
- live_mask: int32 [4096], P(('rcv', 'src')), may hold values 0 or 1
- offsets: int32 [64], replicated, may hold values from 0 to 7936
- block_ids: int32 [2, 16], P(None, 'src'), may hold values from 0 to 31
Outputs:
- stacked: bfloat16 [2, 76, 2048, 4096], P(None, None, 'src', 'rcv')
All inputs are finite; a program needn't handle non-finite values. No bound on the sum of `live_mask` on one device may be relied on, other than what follows from the above.
Results may differ from a plain program's by a relative error of at most 0.0059.
Values may be sent and summed in bfloat16 or wider, within the bound.
A program may use at most 128 MiB of HBM per device.

v0:
```python
import jax
import jax.numpy as jnp
from jax import lax
from jax.sharding import PartitionSpec as P

L = 256
SB = 128
LAGS = 76


def broadcast(value, axis, source):
    kept = jnp.where(lax.axis_index(axis) == source, value, 0).astype(value.dtype)
    return lax.psum(kept, axis)


def build_tables(length, win_count, lag_count):
    sample_axis = jnp.arange(length, dtype=jnp.float32)
    bin_count = length // 2
    bin_axis = jnp.arange(bin_count, dtype=jnp.float32)
    phases = 2.0 * jnp.pi * sample_axis[:, None] * bin_axis[None, :] / length
    taper = 0.5 - 0.5 * jnp.cos(2.0 * jnp.pi * sample_axis / length)
    dft_table = jnp.concatenate(
        [taper[:, None] * jnp.cos(phases), -taper[:, None] * jnp.sin(phases)], axis=1
    ).astype(jnp.bfloat16)
    lag_axis = jnp.arange(lag_count, dtype=jnp.float32)
    weights = jnp.where(bin_axis == 0, 1.0, 2.0).astype(jnp.float32)
    lag_table = (
        weights[:, None]
        * jnp.cos(2.0 * jnp.pi * bin_axis[:, None] * lag_axis[None, :] / length)
        * (2.0 / (win_count * length))
    ).astype(jnp.bfloat16)
    return (dft_table, lag_table)


def transform(live_rec, offsets, dft_table):
    receiver_total = live_rec.shape[0]
    length = dft_table.shape[0]
    win_count = offsets.shape[0]
    windows = jax.vmap(lambda anchor: lax.dynamic_slice_in_dim(live_rec, anchor, length, 1))(
        offsets
    )
    flat_spec = jnp.dot(
        windows.reshape(win_count * receiver_total, length),
        dft_table,
        preferred_element_type=jnp.float32,
    ).astype(jnp.bfloat16)
    bin_count = dft_table.shape[1] // 2
    return (
        flat_spec.reshape(win_count, receiver_total, 2, bin_count)
        .transpose(3, 1, 2, 0)
        .reshape(bin_count, receiver_total, 2 * win_count)
    )


def correlate(source_block, receiver_block, lag_table, src_chan, rcv_chan):
    cross_spectrum = jnp.einsum(
        "mdt,mpt->mdp", source_block, receiver_block, preferred_element_type=jnp.float32
    ).astype(jnp.bfloat16)
    bin_count, src_count, receiver_total = cross_spectrum.shape
    mixed = jnp.dot(
        lag_table.T,
        cross_spectrum.reshape(bin_count, src_count * receiver_total),
        preferred_element_type=jnp.float32,
    )
    mixed = mixed.reshape(-1, src_count, receiver_total)
    self_pair = src_chan[:, None] == rcv_chan[None, :]
    return jnp.where(self_pair[None], 0.0, mixed).astype(jnp.bfloat16)


def local(records, live_mask, offsets, block_ids):
    group_member_count = records.shape[0] * lax.axis_size("src")
    dft_table, lag_table = build_tables(L, offsets.shape[0], LAGS)
    live_rec = records * live_mask[:, None].astype(records.dtype)
    local_spectrum = transform(live_rec, offsets, dft_table)
    receiver_block = lax.all_gather(local_spectrum, "src", axis=1, tiled=True)
    rcv_chan = lax.axis_index("rcv") * group_member_count + jnp.arange(
        group_member_count, dtype=jnp.int32
    )
    results = []
    for turn_index in range(block_ids.shape[0]):
        block_id = block_ids[turn_index, 0]
        first_chan = block_id * SB
        root_rank = first_chan // group_member_count
        beginning = first_chan % group_member_count
        portion = lax.dynamic_slice_in_dim(receiver_block, beginning, SB, 1)
        source_block = broadcast(portion, "rcv", root_rank)
        src_chan = first_chan + jnp.arange(SB, dtype=jnp.int32)
        results.append(correlate(source_block, receiver_block, lag_table, src_chan, rcv_chan))
    return jnp.stack(results)


def solution(mesh):
    in_specs = (P(("rcv", "src"), None), P(("rcv", "src")), P(), P(None, "src"))
    out_specs = P(None, None, "src", "rcv")
    return jax.shard_map(local, mesh=mesh, in_specs=in_specs, out_specs=out_specs, check_vma=False)
```

profile of v0, /device:TPU:32, one launch (start us, length us, event | category | flops | bytes accessed | tf_op | source)
XLA Modules:
  0.0 583.0 jit_solution(16682871106229429336)
XLA Ops:
  8.0 1.0 broadcast_multiply_fusion
  9.0 85.5 %while.1 = (s32[]{:T(128)}, bf16[16,8192]{1,0:T(8,128)(2,1)S(1)}, s32[64,2]{0,1:T(2,128)S(1)}, bf16[64,16,256]{2,1,0:T(8,128)(2,1)S(1)}, s32[]{:T(128)}) while((s32[]{:T(128)}, bf16[16,8192]{1,0:T(8,128)(2,1)S(1)}, s32[64,2]{0,1:T(2,128)S(1)}, bf16[64,16,256]{2,1,0:T(8,128)(2,1)S(1)}, s32[]{:T(128)}) %tuple.23), condition=%wide.while_cond, body=%wide.while_body.sunk | while | flops 2 | bytes 16481 | solution.py:39
  9.7 0.7 bitcast_dynamic-update-slice_fusion.2
  11.0 0.7 bitcast_dynamic-update-slice_fusion.2
  13.7 0.7 bitcast_dynamic-update-slice_fusion.2
  15.0 0.7 bitcast_dynamic-update-slice_fusion.2
  16.3 0.7 bitcast_dynamic-update-slice_fusion.2
  17.7 0.7 bitcast_dynamic-update-slice_fusion.2
  19.0 0.7 bitcast_dynamic-update-slice_fusion.2
  20.3 0.7 bitcast_dynamic-update-slice_fusion.2
  21.7 0.7 bitcast_dynamic-update-slice_fusion.2
  23.0 0.7 bitcast_dynamic-update-slice_fusion.2
  24.4 0.7 bitcast_dynamic-update-slice_fusion.2
  25.7 0.7 bitcast_dynamic-update-slice_fusion.2
  27.0 0.7 bitcast_dynamic-update-slice_fusion.2
  28.4 0.7 bitcast_dynamic-update-slice_fusion.2
  29.7 0.7 bitcast_dynamic-update-slice_fusion.2
  32.4 0.7 bitcast_dynamic-update-slice_fusion.2
  33.7 0.7 bitcast_dynamic-update-slice_fusion.2
  35.0 0.7 bitcast_dynamic-update-slice_fusion.2
  36.4 0.7 bitcast_dynamic-update-slice_fusion.2
  39.1 0.7 bitcast_dynamic-update-slice_fusion.2
  40.4 0.7 bitcast_dynamic-update-slice_fusion.2
  41.7 0.7 bitcast_dynamic-update-slice_fusion.2
  43.1 0.7 bitcast_dynamic-update-slice_fusion.2
  44.4 0.7 bitcast_dynamic-update-slice_fusion.2
  45.7 0.7 bitcast_dynamic-update-slice_fusion.2
  47.1 0.7 bitcast_dynamic-update-slice_fusion.2
  48.4 0.7 bitcast_dynamic-update-slice_fusion.2
  49.7 0.7 bitcast_dynamic-update-slice_fusion.2
  51.1 0.7 bitcast_dynamic-update-slice_fusion.2
  52.4 0.7 bitcast_dynamic-update-slice_fusion.2
  53.8 0.7 bitcast_dynamic-update-slice_fusion.2
  55.1 0.7 bitcast_dynamic-update-slice_fusion.2
  57.8 0.7 bitcast_dynamic-update-slice_fusion.2
  59.1 0.7 bitcast_dynamic-update-slice_fusion.2
  60.4 0.7 bitcast_dynamic-update-slice_fusion.2
  61.8 0.7 bitcast_dynamic-update-slice_fusion.2
  64.4 0.7 bitcast_dynamic-update-slice_fusion.2
  65.8 0.7 bitcast_dynamic-update-slice_fusion.2
  67.1 0.7 bitcast_dynamic-update-slice_fusion.2
  68.5 0.7 bitcast_dynamic-update-slice_fusion.2
  69.8 0.7 bitcast_dynamic-update-slice_fusion.2
  71.1 0.7 bitcast_dynamic-update-slice_fusion.2
  72.5 0.7 bitcast_dynamic-update-slice_fusion.2
  73.8 0.7 bitcast_dynamic-update-slice_fusion.2
  75.1 0.7 bitcast_dynamic-update-slice_fusion.2
  76.5 0.7 bitcast_dynamic-update-slice_fusion.2
  77.8 0.7 bitcast_dynamic-update-slice_fusion.2
  95.8 1.2 copy.10
  97.1 1.3 fusion.21
  99.6 125.3 %all-gather.2.cloned.1.call-done = bf16[128,256,128]{2,1,0:T(8,128)(2,1)} async-done(((bf16[128,16,128]{2,1,0:T(8,128)(2,1)}), bf16[128,256,128]{2,1,0:T(8,128)(2,1)}) %all-gather.2.cloned.1.call-update) | async-done | bytes 8388624 | tf_op jit(solution)/shard_map/all_gather | solution.py:75
  224.9 11.2 %dynamic-slice_select_fusion.1 = (bf16[128,128,128]{2,1,0:T(8,128)(2,1)}, bf16[128,128,128]{2,1,0:T(8,128)(2,1)}) fusion(bf16[128,256,128]{2,1,0:T(8,128)(2,1)} %all-gather.2.cloned.1.call-done, s32[]{:T(128)S(6)} %select_n.63, pred[]{:T(512)S(6)} %eq.58, s32[]{:T(128)S(6)} %select_n.69, pred[]{:T(512)S(6)} %eq.61), kind=kLoop, calls=%fused_computation.10 | loop fusion | flops 4194304 | bytes 16777226 | tf_op jit(solution)/shard_map/jit(_where)/select_n | solution.py:12
  236.3 235.9 %all-reduce.4.cloned.1.call-done = (bf16[128,128,128]{2,1,0:T(8,128)(2,1)}, bf16[128,128,128]{2,1,0:T(8,128)(2,1)}) async-done(((bf16[128,128,128]{2,1,0:T(8,128)(2,1)}, bf16[128,128,128]{2,1,0:T(8,128)(2,1)}), (bf16[128,128,128]{2,1,0:T(8,128)(2,1)}, bf16[128,128,128]{2,1,0:T(8,128)(2,1)})) %all-reduce.4.cloned.1.call-update) | async-done | bytes 8388624 | tf_op jit(solution)/shard_map/psum | solution.py:13
  472.2 10.4 %convolution_convert_fusion.1 = bf16[128,128,256]{2,1,0:T(8,128)(2,1)} fusion(bf16[128,128,128]{2,1,0:T(8,128)(2,1)} %get-tuple-element.22, bf16[128,256,128]{2,1,0:T(8,128)(2,1)} %all-gather.2.cloned.1.call-done), kind=kOutput, calls=%fused_computation.6 | convolution fusion | flops 1077936128 | bytes 20971520 | tf_op jit(solution)/shard_map/mdt,mpt->mdp/dot_general | solution.py:56
  482.6 12.5 %copy.14 = bf16[16,8,128,256]{3,1,2,0:T(8,128)(2,1)} copy(bf16[16,8,128,256]{3,2,1,0:T(8,128)(2,1)} %bitcast.43) | data formatting | bytes 16777216
  495.1 11.3 %copy.11 = bf16[32768,128]{1,0:T(8,128)(2,1)} copy(bf16[32768,128]{0,1:T(8,128)(2,1)} %bitcast.44) | data formatting | bytes 16777216 | tf_op jit(solution)/shard_map/dot_general | solution.py:60
  506.4 10.4 %convolution_convert_fusion = bf16[128,128,256]{2,1,0:T(8,128)(2,1)} fusion(bf16[128,128,128]{2,1,0:T(8,128)(2,1)} %get-tuple-element.21, bf16[128,256,128]{2,1,0:T(8,128)(2,1)} %all-gather.2.cloned.1.call-done), kind=kOutput, calls=%fused_computation.5 | convolution fusion | flops 1077936128 | bytes 20971520 | tf_op jit(solution)/shard_map/mdt,mpt->mdp/dot_general | solution.py:56
  516.8 12.3 %copy.15 = bf16[16,8,128,256]{3,1,2,0:T(8,128)(2,1)} copy(bf16[16,8,128,256]{3,2,1,0:T(8,128)(2,1)} %bitcast.42) | data formatting | bytes 16777216
  529.2 11.9 %copy.12 = bf16[32768,128]{1,0:T(8,128)(2,1)} copy(bf16[32768,128]{0,1:T(8,128)(2,1)} %bitcast.45) | data formatting | bytes 16777216 | tf_op jit(solution)/shard_map/dot_general | solution.py:60
  541.1 9.0 %fusion = bf16[1,76,128,256]{3,1,2,0:T(8,128)(2,1)} fusion(pred[128,256]{1,0:T(8,128)(4,1)S(1)} %get-tuple-element.25, bf16[128,256,128]{2,1,0:T(8,128)(2,1)} %bitcast.40, f32[128]{0:T(128)S(1)} %get-tuple-element.36, f32[128]{0:T(128)S(1)} %get-tuple-element.35), kind=kOutput, calls=%fused_computation.7 | convolution fusion | flops 642563584 | bytes 13403136 | tf_op jit(solution)/shard_map/dot_general | solution.py:60
  550.0 5.5 fusion.1
  555.5 9.0 %pad_maximum_fusion = bf16[2,76,128,256]{3,1,2,0:T(8,128)(2,1)} fusion(bf16[1,76,128,256]{3,1,2,0:T(8,128)(2,1)} %fusion.1, bf16[1,76,128,256]{3,1,2,0:T(8,128)(2,1)} %fusion), kind=kLoop, calls=%fused_computation.2 | loop fusion | flops 4980736 | bytes 19922944 | tf_op jit(solution)/shard_map/stack | solution.py:89
  564.5 11.6 %copy.13 = bf16[2,76,128,256]{3,2,1,0:T(8,128)(2,1)} copy(bf16[2,76,128,256]{3,1,2,0:T(8,128)(2,1)} %pad_maximum_fusion) | data formatting | bytes 19922944 | tf_op jit(solution)/shard_map/stack | solution.py:89
  (165 shorter events, 54.7 us)
Async XLA Ops:
  6.5 218.3 %all-gather.2.cloned.1.call-start = ((), (), s32[]{:S(2)}) async-start(), calls=%async_computation | async-start | bytes 8912896 | tf_op jit(solution)/shard_map/all_gather | solution.py:75
  97.0 375.2 %all-reduce.4.cloned.1.call-start = ((), (), s32[]{:S(2)}) async-start(), calls=%async_computation.1 | async-start | bytes 16777216 | tf_op jit(solution)/shard_map/psum | solution.py:13
  541.1 9.0 %copy-start = (bf16[32768,128]{1,0:T(8,128)(2,1)S(1)}, bf16[32768,128]{1,0:T(8,128)(2,1)}, u32[]{:S(2)}) copy-start(bf16[32768,128]{1,0:T(8,128)(2,1)} %copy.12) | copy-start | bytes 25165828
Sparse Core Ops, SparseCore 0:
  97.1 127.7 all-gather.1
  236.3 235.8 all-reduce.3
where the time goes:
time: 584 us; the launch traced here: 583 us
  waiting for transfers between devices  361 us (62%)
  local copies, waits for them, and re-layouts  148 us (25%)
  matrix products  35.6 us (6%)
  other arithmetic  23.4 us (4%)
  between operations  14.7 us (3%)
    psum x1, waiting for transfers between devices, broadcast(): return lax.psum(kept, axis)  236 us
    all_gather x1, waiting for transfers between devices, local(): receiver_block = lax.all_gather(local_spectrum, 'src', axis=1, tiled=True)  125 us
    gather x192, local copies, waits for them, and re-layouts  85.4 us
    unnamed x4, local copies, waits for them, and re-layouts  24.9 us
    dot_general x2, local copies, waits for them, and re-layouts, correlate(): jnp.dot(lag_table.T, cross_spectrum.reshape(bin_count, src_count * receiv...  23.2 us
    dot_general x2, matrix products, correlate(): jnp.einsum('mdt,mpt->mdp', source_block, receiver_block, preferred_elemen...  20.8 us
    dot_general x2, matrix products, correlate(): jnp.dot(lag_table.T, cross_spectrum.reshape(bin_count, src_count * receiv...  14.5 us
  transfers between devices with their start and end apart: 2, of which 2 were waited for; matrix products, arithmetic and copies ran while one was open for 0% of the time, Pallas kernels for 0%

commit v1 on v0

--- a/solution.py
+++ b/solution.py
@@ -6,6 +6,15 @@
 L = 256
 SB = 128
 LAGS = 76
+find_lane_by_axis = lambda message, a_name: jnp.concatenate(
+    lax.all_to_all(
+        jnp.stack([message for _ in range(lax.psum(1, a_name))]),
+        axis_name=a_name,
+        split_axis=0,
+        concat_axis=0,
+    ),
+    axis=1,
+)
 
 
 def broadcast(value, axis, source):
@@ -72,7 +81,7 @@
     dft_table, lag_table = build_tables(L, offsets.shape[0], LAGS)
     live_rec = records * live_mask[:, None].astype(records.dtype)
     local_spectrum = transform(live_rec, offsets, dft_table)
-    receiver_block = lax.all_gather(local_spectrum, "src", axis=1, tiled=True)
+    receiver_block = find_lane_by_axis(local_spectrum, "src")
     rcv_chan = lax.axis_index("rcv") * group_member_count + jnp.arange(
         group_member_count, dtype=jnp.int32
     )

time: 584 us -> 665 us (1.14)
  waiting for transfers between devices: 361 us -> 416 us
  local copies, waits for them, and re-layouts: 148 us -> 161 us
  starting transfers between devices: 0.04 us -> 9.06 us
    all_to_all x0 -> x1, waiting for transfers between devices: none -> 178 us  [lax.all_to_all(jnp.stack([message for _ in range(lax.psum(1, a_name))]),...]
    all_gather x1 -> x0, waiting for transfers between devices: 125 us -> none  [local(): receiver_block = lax.all_gather(local_spectrum, 'src', axis=1, tiled=True)]
    all_to_all x0 -> x1, starting transfers between devices: none -> 8.77 us  [lax.all_to_all(jnp.stack([message for _ in range(lax.psum(1, a_name))]),...]
    reshape x1, local copies, waits for them, and re-layouts: 1.19 us -> 9.25 us  [jnp.concatenate(lax.all_to_all(jnp.stack([message for _ in range(lax.psum...]
    unnamed x4 -> x6, local copies, waits for them, and re-layouts: 24.9 us -> 25.3 us
where the time goes in v1:
time: 665 us; the launch traced here: 660 us
  waiting for transfers between devices  416 us (63%)
  local copies, waits for them, and re-layouts  161 us (24%)
  matrix products  35.3 us (5%)
  other arithmetic  23.3 us (4%)
  between operations  15 us (2%)
  starting transfers between devices  9.06 us (1%)
    psum x1, waiting for transfers between devices, broadcast(): return lax.psum(kept, axis)  239 us
    all_to_all x1, waiting for transfers between devices, lax.all_to_all(jnp.stack([message for _ in range(lax.psum(1, a_name))]),...  178 us
    gather x192, local copies, waits for them, and re-layouts  85.4 us
    unnamed x6, local copies, waits for them, and re-layouts  25.3 us
    dot_general x2, local copies, waits for them, and re-layouts, correlate(): jnp.dot(lag_table.T, cross_spectrum.reshape(bin_count, src_count * receiv...  23.4 us
    dot_general x2, matrix products, correlate(): jnp.einsum('mdt,mpt->mdp', source_block, receiver_block, preferred_elemen...  20.5 us
    dot_general x2, matrix products, correlate(): jnp.dot(lag_table.T, cross_spectrum.reshape(bin_count, src_count * receiv...  14.5 us
  transfers between devices with their start and end apart: 2, of which 2 were waited for; matrix products, arithmetic and copies ran while one was open for 0% of the time, Pallas kernels for 0%

profile of v1, /device:TPU:32, one launch (start us, length us, event | category | flops | bytes accessed | tf_op | source)
XLA Modules:
  0.0 660.3 jit_solution(5575050207625884485)
XLA Ops:
  8.0 1.0 broadcast_multiply_fusion
  9.0 85.5 %while.1 = (s32[]{:T(128)}, bf16[16,8192]{1,0:T(8,128)(2,1)S(1)}, s32[64,2]{0,1:T(2,128)S(1)}, bf16[64,16,256]{2,1,0:T(8,128)(2,1)S(1)}, s32[]{:T(128)}) while((s32[]{:T(128)}, bf16[16,8192]{1,0:T(8,128)(2,1)S(1)}, s32[64,2]{0,1:T(2,128)S(1)}, bf16[64,16,256]{2,1,0:T(8,128)(2,1)S(1)}, s32[]{:T(128)}) %tuple.23), condition=%wide.while_cond, body=%wide.while_body.sunk | while | flops 2 | bytes 16481 | solution.py:48
  9.7 0.7 bitcast_dynamic-update-slice_fusion.2
  11.0 0.7 bitcast_dynamic-update-slice_fusion.2
  12.3 0.7 bitcast_dynamic-update-slice_fusion.2
  13.7 0.7 bitcast_dynamic-update-slice_fusion.2
  15.0 0.7 bitcast_dynamic-update-slice_fusion.2
  16.3 0.7 bitcast_dynamic-update-slice_fusion.2
  17.7 0.7 bitcast_dynamic-update-slice_fusion.2
  19.0 0.7 bitcast_dynamic-update-slice_fusion.2
  20.3 0.7 bitcast_dynamic-update-slice_fusion.2
  21.7 0.7 bitcast_dynamic-update-slice_fusion.2
  24.4 0.7 bitcast_dynamic-update-slice_fusion.2
  25.7 0.7 bitcast_dynamic-update-slice_fusion.2
  27.0 0.7 bitcast_dynamic-update-slice_fusion.2
  28.4 0.7 bitcast_dynamic-update-slice_fusion.2
  31.0 0.7 bitcast_dynamic-update-slice_fusion.2
  32.4 0.7 bitcast_dynamic-update-slice_fusion.2
  33.7 0.7 bitcast_dynamic-update-slice_fusion.2
  35.0 0.7 bitcast_dynamic-update-slice_fusion.2
  36.4 0.7 bitcast_dynamic-update-slice_fusion.2
  37.7 0.7 bitcast_dynamic-update-slice_fusion.2
  39.1 0.7 bitcast_dynamic-update-slice_fusion.2
  40.4 0.7 bitcast_dynamic-update-slice_fusion.2
  41.7 0.7 bitcast_dynamic-update-slice_fusion.2
  43.1 0.7 bitcast_dynamic-update-slice_fusion.2
  44.4 0.7 bitcast_dynamic-update-slice_fusion.2
  45.7 0.7 bitcast_dynamic-update-slice_fusion.2
  47.1 0.7 bitcast_dynamic-update-slice_fusion.2
  49.7 0.7 bitcast_dynamic-update-slice_fusion.2
  51.1 0.7 bitcast_dynamic-update-slice_fusion.2
  52.4 0.7 bitcast_dynamic-update-slice_fusion.2
  53.8 0.7 bitcast_dynamic-update-slice_fusion.2
  56.4 0.7 bitcast_dynamic-update-slice_fusion.2
  57.8 0.7 bitcast_dynamic-update-slice_fusion.2
  59.1 0.7 bitcast_dynamic-update-slice_fusion.2
  60.4 0.7 bitcast_dynamic-update-slice_fusion.2
  61.8 0.7 bitcast_dynamic-update-slice_fusion.2
  63.1 0.7 bitcast_dynamic-update-slice_fusion.2
  64.4 0.7 bitcast_dynamic-update-slice_fusion.2
  65.8 0.7 bitcast_dynamic-update-slice_fusion.2
  67.1 0.7 bitcast_dynamic-update-slice_fusion.2
  68.5 0.7 bitcast_dynamic-update-slice_fusion.2
  69.8 0.7 bitcast_dynamic-update-slice_fusion.2
  71.1 0.7 bitcast_dynamic-update-slice_fusion.2
  72.5 0.7 bitcast_dynamic-update-slice_fusion.2
  75.1 0.7 bitcast_dynamic-update-slice_fusion.2
  76.5 0.7 bitcast_dynamic-update-slice_fusion.2
  96.2 5.0 stack.12
  101.2 8.8 %all-to-all-start = ((bf16[16,128,16,128]{3,2,1,0:T(8,128)(2,1)}), bf16[16,128,16,128]{3,2,1,0:T(8,128)(2,1)}, u32[]{:S(2)}, u32[]{:S(2)}) async-start(bf16[16,128,16,128]{3,2,1,0:T(8,128)(2,1)} %stack.12), calls=%async_computation | async-start | bytes 16777216 | tf_op jit(solution)/shard_map/all_to_all | solution.py:10
  112.2 177.6 %all-to-all-done = bf16[16,128,16,128]{3,2,1,0:T(8,128)(2,1)} async-done(((bf16[16,128,16,128]{3,2,1,0:T(8,128)(2,1)}), bf16[16,128,16,128]{3,2,1,0:T(8,128)(2,1)}, u32[]{:S(2)}, u32[]{:S(2)}) %all-to-all-start) | async-done | bytes 8388640 | tf_op jit(solution)/shard_map/all_to_all | solution.py:10
  289.8 9.3 %copy.15 = bf16[128,16,16,128]{3,2,1,0:T(8,128)(2,1)} copy(bf16[128,16,16,128]{3,2,0,1:T(8,128)(2,1)} %bitcast.6) | data formatting | bytes 16777216 | tf_op jit(solution)/shard_map/reshape | solution.py:9
  299.1 11.1 %dynamic-slice_select_fusion.1 = (bf16[128,128,128]{2,1,0:T(8,128)(2,1)}, bf16[128,128,128]{2,1,0:T(8,128)(2,1)}) fusion(bf16[128,256,128]{2,1,0:T(8,128)(2,1)} %bitcast.42, s32[]{:T(128)S(6)} %select_n.63, pred[]{:T(512)S(6)} %eq.58, s32[]{:T(128)S(6)} %select_n.69, pred[]{:T(512)S(6)} %eq.61), kind=kLoop, calls=%fused_computation.10 | loop fusion | flops 4194304 | bytes 16777226 | tf_op jit(solution)/shard_map/jit(_where)/select_n | solution.py:21
  310.4 238.6 %all-reduce.4.cloned.1.call-done = (bf16[128,128,128]{2,1,0:T(8,128)(2,1)}, bf16[128,128,128]{2,1,0:T(8,128)(2,1)}) async-done(((bf16[128,128,128]{2,1,0:T(8,128)(2,1)}, bf16[128,128,128]{2,1,0:T(8,128)(2,1)}), (bf16[128,128,128]{2,1,0:T(8,128)(2,1)}, bf16[128,128,128]{2,1,0:T(8,128)(2,1)})) %all-reduce.4.cloned.1.call-update) | async-done | bytes 8388624 | tf_op jit(solution)/shard_map/psum | solution.py:22
  548.9 10.2 %convolution_convert_fusion.1 = bf16[128,128,256]{2,1,0:T(8,128)(2,1)} fusion(bf16[128,128,128]{2,1,0:T(8,128)(2,1)} %get-tuple-element.22, bf16[128,256,128]{2,1,0:T(8,128)(2,1)} %bitcast.43), kind=kOutput, calls=%fused_computation.6 | convolution fusion | flops 1077936128 | bytes 20971520 | tf_op jit(solution)/shard_map/mdt,mpt->mdp/dot_general | solution.py:65
  559.2 12.8 %copy.19 = bf16[16,8,128,256]{3,1,2,0:T(8,128)(2,1)} copy(bf16[16,8,128,256]{3,2,1,0:T(8,128)(2,1)} %bitcast.48) | data formatting | bytes 16777216
  572.0 11.9 %copy.16 = bf16[32768,128]{1,0:T(8,128)(2,1)} copy(bf16[32768,128]{0,1:T(8,128)(2,1)} %bitcast.49) | data formatting | bytes 16777216 | tf_op jit(solution)/shard_map/dot_general | solution.py:69
  583.9 10.2 %convolution_convert_fusion = bf16[128,128,256]{2,1,0:T(8,128)(2,1)} fusion(bf16[128,128,128]{2,1,0:T(8,128)(2,1)} %get-tuple-element.21, bf16[128,256,128]{2,1,0:T(8,128)(2,1)} %bitcast.44), kind=kOutput, calls=%fused_computation.5 | convolution fusion | flops 1077936128 | bytes 20971520 | tf_op jit(solution)/shard_map/mdt,mpt->mdp/dot_general | solution.py:65
  594.2 12.5 %copy.20 = bf16[16,8,128,256]{3,1,2,0:T(8,128)(2,1)} copy(bf16[16,8,128,256]{3,2,1,0:T(8,128)(2,1)} %bitcast.47) | data formatting | bytes 16777216
  606.7 11.5 %copy.17 = bf16[32768,128]{1,0:T(8,128)(2,1)} copy(bf16[32768,128]{0,1:T(8,128)(2,1)} %bitcast.50) | data formatting | bytes 16777216 | tf_op jit(solution)/shard_map/dot_general | solution.py:69
  618.2 9.0 %fusion = bf16[1,76,128,256]{3,1,2,0:T(8,128)(2,1)} fusion(pred[128,256]{1,0:T(8,128)(4,1)S(1)} %get-tuple-element.25, bf16[128,256,128]{2,1,0:T(8,128)(2,1)} %bitcast.45, f32[128]{0:T(128)S(1)} %get-tuple-element.36, f32[128]{0:T(128)S(1)} %get-tuple-element.35), kind=kOutput, calls=%fused_computation.7 | convolution fusion | flops 642563584 | bytes 13403136 | tf_op jit(solution)/shard_map/dot_general | solution.py:69
  627.2 5.5 fusion.1
  632.7 9.0 %pad_maximum_fusion = bf16[2,76,128,256]{3,1,2,0:T(8,128)(2,1)} fusion(bf16[1,76,128,256]{3,1,2,0:T(8,128)(2,1)} %fusion.1, bf16[1,76,128,256]{3,1,2,0:T(8,128)(2,1)} %fusion), kind=kLoop, calls=%fused_computation.2 | loop fusion | flops 4980736 | bytes 19922944 | tf_op jit(solution)/shard_map/stack | solution.py:98
  641.7 11.6 %copy.18 = bf16[2,76,128,256]{3,2,1,0:T(8,128)(2,1)} copy(bf16[2,76,128,256]{3,1,2,0:T(8,128)(2,1)} %pad_maximum_fusion) | data formatting | bytes 19922944 | tf_op jit(solution)/shard_map/stack | solution.py:98
  (168 shorter events, 56.7 us)
Async XLA Ops:
  101.2 9.1 %copy-start.1 = (s32[2,1]{0,1:T(1,128)S(1)}, s32[2,1]{0,1:T(1,128)}, u32[]{:S(2)}) copy-start(s32[2,1]{0,1:T(1,128)} %param.7) | copy-start | bytes 28
  101.2 188.6 %all-to-all-start = ((bf16[16,128,16,128]{3,2,1,0:T(8,128)(2,1)}), bf16[16,128,16,128]{3,2,1,0:T(8,128)(2,1)}, u32[]{:S(2)}, u32[]{:S(2)}) async-start(bf16[16,128,16,128]{3,2,1,0:T(8,128)(2,1)} %stack.12), calls=%async_computation | async-start | bytes 16777216 | tf_op jit(solution)/shard_map/all_to_all | solution.py:10
  110.0 438.9 %all-reduce.4.cloned.1.call-start = ((), (), s32[]{:S(2)}) async-start(), calls=%async_computation.1 | async-start | bytes 16777216 | tf_op jit(solution)/shard_map/psum | solution.py:22
  618.2 9.0 %copy-start = (bf16[32768,128]{1,0:T(8,128)(2,1)S(1)}, bf16[32768,128]{1,0:T(8,128)(2,1)}, u32[]{:S(2)}) copy-start(bf16[32768,128]{1,0:T(8,128)(2,1)} %copy.17) | copy-start | bytes 25165828
Sparse Core Ops, SparseCore 0:
  310.3 238.5 all-reduce.3
